TPU v7x, 32 devices: a whole 2x2x4 slice. The times are simulated.
32 devices in a mesh: groups: 2 (over y), ctx: 4 (over z), head: 4 (over x, core).
Axes of the slice: x: 2, y: 2, z: 4, core: 2. Of those that a mesh axis runs over, the one named last changes fastest.
Arguments:
- queries: bfloat16 [65536, 2048], P(('groups', 'ctx'), 'head'), parts along dimension 0, may hold values from -9 to 9
- keys: bfloat16 [65536, 1024], P(('groups', 'ctx'), 'head'), parts along dimension 0, may hold values from -6 to 6
- values: bfloat16 [65536, 1024], P(('groups', 'ctx'), 'head'), parts along dimension 0, may hold values from -6 to 6
- doc_lengths: int32 [32], P('groups'), parts along dimension 0, may hold values from 1 to 8192, 32768 in all
- live_blocks: int32 [8], P('groups'), parts along dimension 0, may hold values from 1 to 16, as said below
Outputs:
- attended: bfloat16 [65536, 2048], P(('groups', 'ctx'), 'head'), parts along dimension 0
- log_norm: float32 [32, 32768], P(('groups', 'head'), 'ctx'), parts along dimension 0
There are 2 independent parts, one for each index of `groups`. A program takes and returns all parts, laid end to end along the dimension named above; each array names one. Nothing has to cross between parts.
Inputs may be any that keep to these rules, and one draw needn't show every extreme that they name: `live_blocks`: shards are paired heavy with light: for every shard s below 2, one of shards s and s + 2 has 16 scored blocks and the other fewer than 16.
All inputs are finite; a program needn't handle non-finite values.
Results may differ from a plain program's by a relative error of at most 0.0043.
Values may be sent and summed in bfloat16 or wider, within the bound.
A program may use at most 128 MiB of HBM per device.

v0:
```python
import jax
import jax.numpy as jnp
from jax import lax
from jax.sharding import PartitionSpec as P

HD = 128
W = 1024
BLK = 512


score_scale = 168.0 ** (-0.5)


def from_behind(shard, axis, by):
    devices = lax.axis_size(axis)
    pairs = [(i, i + by) for i in range(devices) if 0 <= i + by < devices]
    return lax.ppermute(shard, axis, pairs)


def doc_index(starts, positions):
    return jnp.sum((starts[None, :] <= positions[:, None]).astype(jnp.int32), axis=1) - 1


def attend_block(query_src, key_src, value_src, starts, block_idx, global_base):
    query_width = query_src.shape[1]
    key_width = key_src.shape[1]
    kv_heads = key_width // HD
    span = W + BLK
    row_start = block_idx * BLK
    query_blk = lax.dynamic_slice_in_dim(query_src, row_start, BLK, 0)
    key_blk = lax.dynamic_slice_in_dim(key_src, row_start, span, 0)
    value_blk = lax.dynamic_slice_in_dim(value_src, row_start, span, 0)
    scores = (
        jnp.einsum(
            "qhgd,khd->hgqk",
            query_blk.reshape(BLK, kv_heads, 2, HD),
            key_blk.reshape(span, kv_heads, HD),
            preferred_element_type=jnp.float32,
        )
        * score_scale
    )
    global_start = global_base + row_start
    query_pos = global_start + jnp.arange(BLK, dtype=jnp.int32)
    key_pos = global_start - W + jnp.arange(span, dtype=jnp.int32)
    allowed = doc_index(starts, key_pos)[None, :] == doc_index(starts, query_pos)[:, None]
    allowed = (
        allowed
        & (key_pos[None, :] <= query_pos[:, None])
        & (key_pos[None, :] > query_pos[:, None] - W)
        & (key_pos[None, :] >= 0)
    )
    allowed = allowed[None, None]
    top = jnp.max(jnp.where(allowed, scores, -jnp.inf), axis=-1, keepdims=True)
    probs = jnp.where(allowed, jnp.exp(scores - top), 0.0)
    total = jnp.sum(probs, axis=-1)
    weights = probs.astype(jnp.bfloat16)
    mixed = jnp.einsum(
        "hgqk,khd->qhgd",
        weights,
        value_blk.reshape(span, kv_heads, HD),
        preferred_element_type=jnp.float32,
    )
    mixed = mixed / jnp.transpose(total, (2, 0, 1))[..., None]
    attended = mixed.astype(jnp.bfloat16).reshape(BLK, query_width)
    log_norm = (top[..., 0] + jnp.log(total)).reshape(2 * kv_heads, BLK)
    return (attended, log_norm)


def run_blocks(query_src, key_src, value_src, starts, block_count, global_base):
    src_rows = query_src.shape[0]
    query_width = query_src.shape[1]
    heads_here = query_width // HD
    out_init = jnp.zeros((src_rows, query_width), jnp.bfloat16)
    norm_init = jnp.zeros((heads_here, src_rows), jnp.float32)

    def step_fn(index, carry):
        out_buf, norm_buf = carry
        attended, log_norm = attend_block(query_src, key_src, value_src, starts, index, global_base)
        out_buf = lax.dynamic_update_slice(out_buf, attended, (index * BLK, 0))
        norm_buf = lax.dynamic_update_slice(norm_buf, log_norm, (0, index * BLK))
        return (out_buf, norm_buf)

    return lax.fori_loop(jnp.int32(0), block_count, step_fn, (out_init, norm_init))


def local(queries, keys, values, doc_lengths, live_blocks):
    shard_rows = queries.shape[0]
    own_shard = lax.axis_index("ctx")
    prev_keys, prev_values = from_behind(
        (keys[shard_rows - W :], values[shard_rows - W :]), "ctx", 1
    )
    keys_ext = jnp.concatenate([prev_keys, keys], axis=0)
    values_ext = jnp.concatenate([prev_values, values], axis=0)
    starts = jnp.cumsum(doc_lengths) - doc_lengths
    own_count = live_blocks[own_shard]
    own_base = own_shard * shard_rows
    attended, log_norm = run_blocks(queries, keys_ext, values_ext, starts, own_count, own_base)
    return (attended, log_norm)


def solution(mesh):
    in_specs = (
        P(("groups", "ctx"), "head"),
        P(("groups", "ctx"), "head"),
        P(("groups", "ctx"), "head"),
        P("groups"),
        P("groups"),
    )
    out_specs = (P(("groups", "ctx"), "head"), P(("groups", "head"), "ctx"))
    return jax.shard_map(local, mesh=mesh, in_specs=in_specs, out_specs=out_specs, check_vma=False)
```

profile of v0, /device:TPU:0, one launch (start us, length us, event | category | flops | bytes accessed | tf_op | source)
XLA Modules:
  0.0 275.2 jit_solution(8060140553816568050)
XLA Ops:
  0.7 6.4 %copy.28 = bf16[8192,256]{0,1:T(8,128)(2,1)} copy(bf16[8192,256]{1,0:T(8,128)(2,1)} %param.8) | data formatting | bytes 8388608 | tf_op args[1]
  8.2 5.0 %collective-permute-start.1 = (bf16[1024,256]{0,1:T(8,128)(2,1)S(1)}, bf16[1024,256]{0,1:T(8,128)(2,1)S(1)}, u32[]{:S(2)}, u32[]{:S(2)}) collective-permute-start(bf16[1024,256]{0,1:T(8,128)(2,1)S(1)} %slice.9), channel_id=1, source_target_pairs={{0,4},{4,8},{8,12},{1,5},{5,9},{9,13},{2,6},{6,10},{10,14},{3,7},{... | collective-permute-start | bytes 1572872 | tf_op jit(solution)/shard_map/ppermute | solution.py:17
  13.2 6.3 %copy.25 = bf16[8192,256]{0,1:T(8,128)(2,1)} copy(bf16[8192,256]{1,0:T(8,128)(2,1)} %param.9) | data formatting | bytes 8388608 | tf_op args[2]
  20.6 3.5 %collective-permute-start = (bf16[1024,256]{0,1:T(8,128)(2,1)S(1)}, bf16[1024,256]{0,1:T(8,128)(2,1)S(1)}, u32[]{:S(2)}, u32[]{:S(2)}) collective-permute-start(bf16[1024,256]{0,1:T(8,128)(2,1)S(1)} %slice.8), channel_id=1, source_target_pairs={{0,4},{4,8},{8,12},{1,5},{5,9},{9,13},{2,6},{6,10},{10,14},{3,7},{... | collective-permute-start | bytes 1572872 | tf_op jit(solution)/shard_map/ppermute | solution.py:17
  25.0 4.9 %pad_maximum_fusion.1 = bf16[9216,256]{0,1:T(8,128)(2,1)} fusion(bf16[8192,256]{0,1:T(8,128)(2,1)} %copy.28, bf16[1024,256]{0,1:T(8,128)(2,1)S(1)} %collective-permute-done.1), kind=kLoop, calls=%fused_computation.29 | loop fusion | flops 9437184 | bytes 9437184 | tf_op jit(solution)/shard_map/concatenate | solution.py:92
  29.9 5.6 %collective-permute-done = bf16[1024,256]{0,1:T(8,128)(2,1)S(1)} collective-permute-done((bf16[1024,256]{0,1:T(8,128)(2,1)S(1)}, bf16[1024,256]{0,1:T(8,128)(2,1)S(1)}, u32[]{:S(2)}, u32[]{:S(2)}) %collective-permute-start) | collective-permute-done | bytes 524320 | tf_op jit(solution)/shard_map/ppermute | solution.py:17
  38.1 3.9 %broadcast_in_dim.51.clone = bf16[8192,512]{1,0:T(8,128)(2,1)} broadcast(bf16[]{:T(256)} %constant.75.clone.1), dimensions={} | broadcast | bytes 8388610 | tf_op jit(solution)/shard_map/broadcast_in_dim | solution.py:73
  42.1 232.5 %while.15 = (s32[]{:T(128)}, bf16[8192,512]{1,0:T(8,128)(2,1)}, f32[4,8192]{1,0:T(4,128)S(1)}, s32[]{:T(128)}, bf16[9216,256]{0,1:T(8,128)(2,1)}, /*index=5*/s32...) while((s32[]{:T(128)}, bf16[8192,512]{1,0:T(8,128)(2,1)}, ...), condition=%wide.region_6.7_spmd, body=%wide.region_1.6_spmd.sunk | while | flops 1650560512 | bytes 51019144 | solution.py:83
  52.4 3.1 %divide_convert_fusion.2 = bf16[512,2,2,128]{0,3,2,1:T(8,128)(2,1)S(1)} fusion(bf16[1536,2,128,1]{0,2,3,1:T(8,128)(2,1)S(1)} %bitcast.64, f32[2,1536,512,2]{2,1,3,0:T(8,128)S(1)} %get-tuple-element.266, f32[2,2,512]{2,1,0:T(2,128)S(1)} %get-tuple-element.267, pred[512,1536]{0,1:T(8,128)(4,1)S(1)} %and_and_fusion.2, f32[512,2,2]{0,2,1:T(2,128)S(1)} %bitcast.68), kind=kOutput, calls=%fused_computation.11.clone.1 | convolution fusion | flops 818413568 | bytes 14696448 | tf_op jit(solution)/shard_map/while/body/hgqk,khd->qhgd/dot_general | solution.py:57
  66.9 3.1 %divide_convert_fusion.2 = bf16[512,2,2,128]{0,3,2,1:T(8,128)(2,1)S(1)} fusion(bf16[1536,2,128,1]{0,2,3,1:T(8,128)(2,1)S(1)} %bitcast.64, f32[2,1536,512,2]{2,1,3,0:T(8,128)S(1)} %get-tuple-element.266, f32[2,2,512]{2,1,0:T(2,128)S(1)} %get-tuple-element.267, pred[512,1536]{0,1:T(8,128)(4,1)S(1)} %and_and_fusion.2, f32[512,2,2]{0,2,1:T(2,128)S(1)} %bitcast.68), kind=kOutput, calls=%fused_computation.11.clone.1 | convolution fusion | flops 818413568 | bytes 14696448 | tf_op jit(solution)/shard_map/while/body/hgqk,khd->qhgd/dot_general | solution.py:57
  81.4 3.1 %divide_convert_fusion.2 = bf16[512,2,2,128]{0,3,2,1:T(8,128)(2,1)S(1)} fusion(bf16[1536,2,128,1]{0,2,3,1:T(8,128)(2,1)S(1)} %bitcast.64, f32[2,1536,512,2]{2,1,3,0:T(8,128)S(1)} %get-tuple-element.266, f32[2,2,512]{2,1,0:T(2,128)S(1)} %get-tuple-element.267, pred[512,1536]{0,1:T(8,128)(4,1)S(1)} %and_and_fusion.2, f32[512,2,2]{0,2,1:T(2,128)S(1)} %bitcast.68), kind=kOutput, calls=%fused_computation.11.clone.1 | convolution fusion | flops 818413568 | bytes 14696448 | tf_op jit(solution)/shard_map/while/body/hgqk,khd->qhgd/dot_general | solution.py:57
  95.9 3.1 %divide_convert_fusion.2 = bf16[512,2,2,128]{0,3,2,1:T(8,128)(2,1)S(1)} fusion(bf16[1536,2,128,1]{0,2,3,1:T(8,128)(2,1)S(1)} %bitcast.64, f32[2,1536,512,2]{2,1,3,0:T(8,128)S(1)} %get-tuple-element.266, f32[2,2,512]{2,1,0:T(2,128)S(1)} %get-tuple-element.267, pred[512,1536]{0,1:T(8,128)(4,1)S(1)} %and_and_fusion.2, f32[512,2,2]{0,2,1:T(2,128)S(1)} %bitcast.68), kind=kOutput, calls=%fused_computation.11.clone.1 | convolution fusion | flops 818413568 | bytes 14696448 | tf_op jit(solution)/shard_map/while/body/hgqk,khd->qhgd/dot_general | solution.py:57
  110.3 3.1 %divide_convert_fusion.2 = bf16[512,2,2,128]{0,3,2,1:T(8,128)(2,1)S(1)} fusion(bf16[1536,2,128,1]{0,2,3,1:T(8,128)(2,1)S(1)} %bitcast.64, f32[2,1536,512,2]{2,1,3,0:T(8,128)S(1)} %get-tuple-element.266, f32[2,2,512]{2,1,0:T(2,128)S(1)} %get-tuple-element.267, pred[512,1536]{0,1:T(8,128)(4,1)S(1)} %and_and_fusion.2, f32[512,2,2]{0,2,1:T(2,128)S(1)} %bitcast.68), kind=kOutput, calls=%fused_computation.11.clone.1 | convolution fusion | flops 818413568 | bytes 14696448 | tf_op jit(solution)/shard_map/while/body/hgqk,khd->qhgd/dot_general | solution.py:57
  124.8 3.1 %divide_convert_fusion.2 = bf16[512,2,2,128]{0,3,2,1:T(8,128)(2,1)S(1)} fusion(bf16[1536,2,128,1]{0,2,3,1:T(8,128)(2,1)S(1)} %bitcast.64, f32[2,1536,512,2]{2,1,3,0:T(8,128)S(1)} %get-tuple-element.266, f32[2,2,512]{2,1,0:T(2,128)S(1)} %get-tuple-element.267, pred[512,1536]{0,1:T(8,128)(4,1)S(1)} %and_and_fusion.2, f32[512,2,2]{0,2,1:T(2,128)S(1)} %bitcast.68), kind=kOutput, calls=%fused_computation.11.clone.1 | convolution fusion | flops 818413568 | bytes 14696448 | tf_op jit(solution)/shard_map/while/body/hgqk,khd->qhgd/dot_general | solution.py:57
  139.3 3.1 %divide_convert_fusion.2 = bf16[512,2,2,128]{0,3,2,1:T(8,128)(2,1)S(1)} fusion(bf16[1536,2,128,1]{0,2,3,1:T(8,128)(2,1)S(1)} %bitcast.64, f32[2,1536,512,2]{2,1,3,0:T(8,128)S(1)} %get-tuple-element.266, f32[2,2,512]{2,1,0:T(2,128)S(1)} %get-tuple-element.267, pred[512,1536]{0,1:T(8,128)(4,1)S(1)} %and_and_fusion.2, f32[512,2,2]{0,2,1:T(2,128)S(1)} %bitcast.68), kind=kOutput, calls=%fused_computation.11.clone.1 | convolution fusion | flops 818413568 | bytes 14696448 | tf_op jit(solution)/shard_map/while/body/hgqk,khd->qhgd/dot_general | solution.py:57
  153.8 3.1 %divide_convert_fusion.2 = bf16[512,2,2,128]{0,3,2,1:T(8,128)(2,1)S(1)} fusion(bf16[1536,2,128,1]{0,2,3,1:T(8,128)(2,1)S(1)} %bitcast.64, f32[2,1536,512,2]{2,1,3,0:T(8,128)S(1)} %get-tuple-element.266, f32[2,2,512]{2,1,0:T(2,128)S(1)} %get-tuple-element.267, pred[512,1536]{0,1:T(8,128)(4,1)S(1)} %and_and_fusion.2, f32[512,2,2]{0,2,1:T(2,128)S(1)} %bitcast.68), kind=kOutput, calls=%fused_computation.11.clone.1 | convolution fusion | flops 818413568 | bytes 14696448 | tf_op jit(solution)/shard_map/while/body/hgqk,khd->qhgd/dot_general | solution.py:57
  168.3 3.1 %divide_convert_fusion.2 = bf16[512,2,2,128]{0,3,2,1:T(8,128)(2,1)S(1)} fusion(bf16[1536,2,128,1]{0,2,3,1:T(8,128)(2,1)S(1)} %bitcast.64, f32[2,1536,512,2]{2,1,3,0:T(8,128)S(1)} %get-tuple-element.266, f32[2,2,512]{2,1,0:T(2,128)S(1)} %get-tuple-element.267, pred[512,1536]{0,1:T(8,128)(4,1)S(1)} %and_and_fusion.2, f32[512,2,2]{0,2,1:T(2,128)S(1)} %bitcast.68), kind=kOutput, calls=%fused_computation.11.clone.1 | convolution fusion | flops 818413568 | bytes 14696448 | tf_op jit(solution)/shard_map/while/body/hgqk,khd->qhgd/dot_general | solution.py:57
  182.8 3.1 %divide_convert_fusion.2 = bf16[512,2,2,128]{0,3,2,1:T(8,128)(2,1)S(1)} fusion(bf16[1536,2,128,1]{0,2,3,1:T(8,128)(2,1)S(1)} %bitcast.64, f32[2,1536,512,2]{2,1,3,0:T(8,128)S(1)} %get-tuple-element.266, f32[2,2,512]{2,1,0:T(2,128)S(1)} %get-tuple-element.267, pred[512,1536]{0,1:T(8,128)(4,1)S(1)} %and_and_fusion.2, f32[512,2,2]{0,2,1:T(2,128)S(1)} %bitcast.68), kind=kOutput, calls=%fused_computation.11.clone.1 | convolution fusion | flops 818413568 | bytes 14696448 | tf_op jit(solution)/shard_map/while/body/hgqk,khd->qhgd/dot_general | solution.py:57
  197.3 3.1 %divide_convert_fusion.2 = bf16[512,2,2,128]{0,3,2,1:T(8,128)(2,1)S(1)} fusion(bf16[1536,2,128,1]{0,2,3,1:T(8,128)(2,1)S(1)} %bitcast.64, f32[2,1536,512,2]{2,1,3,0:T(8,128)S(1)} %get-tuple-element.266, f32[2,2,512]{2,1,0:T(2,128)S(1)} %get-tuple-element.267, pred[512,1536]{0,1:T(8,128)(4,1)S(1)} %and_and_fusion.2, f32[512,2,2]{0,2,1:T(2,128)S(1)} %bitcast.68), kind=kOutput, calls=%fused_computation.11.clone.1 | convolution fusion | flops 818413568 | bytes 14696448 | tf_op jit(solution)/shard_map/while/body/hgqk,khd->qhgd/dot_general | solution.py:57
  211.8 3.1 %divide_convert_fusion.2 = bf16[512,2,2,128]{0,3,2,1:T(8,128)(2,1)S(1)} fusion(bf16[1536,2,128,1]{0,2,3,1:T(8,128)(2,1)S(1)} %bitcast.64, f32[2,1536,512,2]{2,1,3,0:T(8,128)S(1)} %get-tuple-element.266, f32[2,2,512]{2,1,0:T(2,128)S(1)} %get-tuple-element.267, pred[512,1536]{0,1:T(8,128)(4,1)S(1)} %and_and_fusion.2, f32[512,2,2]{0,2,1:T(2,128)S(1)} %bitcast.68), kind=kOutput, calls=%fused_computation.11.clone.1 | convolution fusion | flops 818413568 | bytes 14696448 | tf_op jit(solution)/shard_map/while/body/hgqk,khd->qhgd/dot_general | solution.py:57
  226.3 3.1 %divide_convert_fusion.2 = bf16[512,2,2,128]{0,3,2,1:T(8,128)(2,1)S(1)} fusion(bf16[1536,2,128,1]{0,2,3,1:T(8,128)(2,1)S(1)} %bitcast.64, f32[2,1536,512,2]{2,1,3,0:T(8,128)S(1)} %get-tuple-element.266, f32[2,2,512]{2,1,0:T(2,128)S(1)} %get-tuple-element.267, pred[512,1536]{0,1:T(8,128)(4,1)S(1)} %and_and_fusion.2, f32[512,2,2]{0,2,1:T(2,128)S(1)} %bitcast.68), kind=kOutput, calls=%fused_computation.11.clone.1 | convolution fusion | flops 818413568 | bytes 14696448 | tf_op jit(solution)/shard_map/while/body/hgqk,khd->qhgd/dot_general | solution.py:57
  240.8 3.1 %divide_convert_fusion.2 = bf16[512,2,2,128]{0,3,2,1:T(8,128)(2,1)S(1)} fusion(bf16[1536,2,128,1]{0,2,3,1:T(8,128)(2,1)S(1)} %bitcast.64, f32[2,1536,512,2]{2,1,3,0:T(8,128)S(1)} %get-tuple-element.266, f32[2,2,512]{2,1,0:T(2,128)S(1)} %get-tuple-element.267, pred[512,1536]{0,1:T(8,128)(4,1)S(1)} %and_and_fusion.2, f32[512,2,2]{0,2,1:T(2,128)S(1)} %bitcast.68), kind=kOutput, calls=%fused_computation.11.clone.1 | convolution fusion | flops 818413568 | bytes 14696448 | tf_op jit(solution)/shard_map/while/body/hgqk,khd->qhgd/dot_general | solution.py:57
  255.3 3.1 %divide_convert_fusion.2 = bf16[512,2,2,128]{0,3,2,1:T(8,128)(2,1)S(1)} fusion(bf16[1536,2,128,1]{0,2,3,1:T(8,128)(2,1)S(1)} %bitcast.64, f32[2,1536,512,2]{2,1,3,0:T(8,128)S(1)} %get-tuple-element.266, f32[2,2,512]{2,1,0:T(2,128)S(1)} %get-tuple-element.267, pred[512,1536]{0,1:T(8,128)(4,1)S(1)} %and_and_fusion.2, f32[512,2,2]{0,2,1:T(2,128)S(1)} %bitcast.68), kind=kOutput, calls=%fused_computation.11.clone.1 | convolution fusion | flops 818413568 | bytes 14696448 | tf_op jit(solution)/shard_map/while/body/hgqk,khd->qhgd/dot_general | solution.py:57
  269.8 3.1 %divide_convert_fusion.2 = bf16[512,2,2,128]{0,3,2,1:T(8,128)(2,1)S(1)} fusion(bf16[1536,2,128,1]{0,2,3,1:T(8,128)(2,1)S(1)} %bitcast.64, f32[2,1536,512,2]{2,1,3,0:T(8,128)S(1)} %get-tuple-element.266, f32[2,2,512]{2,1,0:T(2,128)S(1)} %get-tuple-element.267, pred[512,1536]{0,1:T(8,128)(4,1)S(1)} %and_and_fusion.2, f32[512,2,2]{0,2,1:T(2,128)S(1)} %bitcast.68), kind=kOutput, calls=%fused_computation.11.clone.1 | convolution fusion | flops 818413568 | bytes 14696448 | tf_op jit(solution)/shard_map/while/body/hgqk,khd->qhgd/dot_general | solution.py:57
  (306 shorter events, 177.5 us)
Async XLA Ops:
  0.6 23.4 %copy-start.2 = (s32[16]{0:T(128)S(1)}, s32[16]{0:T(128)}, u32[]{:S(2)}) copy-start(s32[16]{0:T(128)} %param.10) | copy-start | bytes 196
  0.6 23.7 %copy-start.3 = (s32[4]{0:T(128)S(1)}, s32[4]{0:T(128)}, u32[]{:S(2)}) copy-start(s32[4]{0:T(128)} %param.11) | copy-start | bytes 52
  8.2 16.8 %collective-permute-start.1 = (bf16[1024,256]{0,1:T(8,128)(2,1)S(1)}, bf16[1024,256]{0,1:T(8,128)(2,1)S(1)}, u32[]{:S(2)}, u32[]{:S(2)}) collective-permute-start(bf16[1024,256]{0,1:T(8,128)(2,1)S(1)} %slice.9), channel_id=1, source_target_pairs={{0,4},{4,8},{8,12},{1,5},{5,9},{9,13},{2,6},{6,10},{10,14},{3,7},{... | collective-permute-start | bytes 1572872 | tf_op jit(solution)/shard_map/ppermute | solution.py:17
  20.6 15.0 %collective-permute-start = (bf16[1024,256]{0,1:T(8,128)(2,1)S(1)}, bf16[1024,256]{0,1:T(8,128)(2,1)S(1)}, u32[]{:S(2)}, u32[]{:S(2)}) collective-permute-start(bf16[1024,256]{0,1:T(8,128)(2,1)S(1)} %slice.8), channel_id=1, source_target_pairs={{0,4},{4,8},{8,12},{1,5},{5,9},{9,13},{2,6},{6,10},{10,14},{3,7},{... | collective-permute-start | bytes 1572872 | tf_op jit(solution)/shard_map/ppermute | solution.py:17
  24.3 11.2 %copy-start = (bf16[8192,256]{0,1:T(8,128)(2,1)S(1)}, bf16[8192,256]{0,1:T(8,128)(2,1)}, u32[]{:S(2)}) copy-start(bf16[8192,256]{0,1:T(8,128)(2,1)} %copy.25) | copy-start | bytes 12582916
  274.6 0.7 copy-start.1
where the time goes:
time: 277 us; the launch traced here: 275 us
  matrix products  86.6 us (31%)
  local copies, waits for them, and re-layouts  81.9 us (30%)
  other arithmetic  79.5 us (29%)
  loops' own time  12.4 us (4%)
  starting transfers between devices  8.47 us (3%)
  waiting for transfers between devices  5.61 us (2%)
    dot_general x16, matrix products, attend_block(): jnp.einsum('hgqk,khd->qhgd', weights, value_blk.reshape(span, kv_heads, H...  48.9 us
    reduce_sum x16, other arithmetic, attend_block(): total = jnp.sum(probs, axis=-1)  43.7 us
    dot_general x16, matrix products, attend_block(): jnp.einsum('qhgd,khd->hgqk', query_blk.reshape(BLK, kv_heads, 2, HD), key...  37.7 us
    and x16, other arithmetic, attend_block(): allowed & (key_pos[None, :] <= query_pos[:, None])  24.6 us
    dynamic_slice x16, local copies, waits for them, and re-layouts, attend_block(): key_blk = lax.dynamic_slice_in_dim(key_src, row_start, span, 0)  23.7 us
    dynamic_slice x32, local copies, waits for them, and re-layouts, attend_block(): query_blk = lax.dynamic_slice_in_dim(query_src, row_start, BLK, 0)  20.7 us
    dynamic_update_slice x32, local copies, waits for them, and re-layouts, step_fn(): out_buf = lax.dynamic_update_slice(out_buf, attended, (index * BLK, 0))  16.7 us
    unnamed x10, local copies, waits for them, and re-layouts  13.4 us
  transfers between devices with their start and end apart: 2, of which 1 were waited for; matrix products, arithmetic and copies ran while one was open for 5% of the time, Pallas kernels for 0%

commit v1 on v0

v1 whole, which is shorter than its diff:
```python
import functools
import math

import jax
import jax.numpy as jnp
from jax import lax
from jax.experimental import pallas as pl
from jax.experimental.pallas import tpu as pltpu
from jax.sharding import PartitionSpec as P

HD = 128
W = 1024
BLK = 512
TILE = 256
SPAN = W // TILE + 1

score_scale = 168.0 ** (-0.5)
log2_scale = score_scale * math.log2(math.e)
MASKED = -1e30


def from_behind(shard, axis, by):
    devices = lax.axis_size(axis)
    pairs = [(i, i + by) for i in range(devices) if 0 <= i + by < devices]
    return lax.ppermute(shard, axis, pairs)


def kernel(first, aliased, info, lengths, q_ref, k_ref, v_ref, pk_ref, pv_ref, *rest):
    out_ref, norm_ref, kbuf, vbuf = rest[2:] if aliased else rest
    step = pl.program_id(0)
    tile = step + first
    live = tile < info[1] * (BLK // TILE)
    kv_heads = k_ref.shape[1] // HD
    docs = lengths.shape[0]

    @pl.when(step == 0)
    def _():
        kbuf[:W, :] = pk_ref[...]
        vbuf[:, :W] = pv_ref[...].T

    @pl.when(jnp.logical_not(live))
    def _():
        out_ref[...] = jnp.zeros_like(out_ref)
        norm_ref[...] = jnp.zeros_like(norm_ref)

    @pl.when(live)
    def _():
        off = pl.multiple_of(step * TILE, TILE)
        kbuf[pl.ds(pl.multiple_of(off + W, TILE), TILE), :] = k_ref[...]
        vbuf[:, pl.ds(pl.multiple_of(off + W, TILE), TILE)] = v_ref[...].T

        t0 = info[0] + tile * TILE
        lane = lax.broadcasted_iota(jnp.int32, (1, TILE), 1)
        pos = t0 + lane
        doc_row = jnp.zeros((1, TILE), jnp.int32)
        doc_first = jnp.int32(0)
        doc_last = jnp.int32(0)
        start = jnp.int32(0)
        for i in range(docs):
            doc_row = jnp.where(start <= pos, start, doc_row)
            doc_first = jnp.where(start <= t0, start, doc_first)
            doc_last = jnp.where(start <= t0 + TILE - 1, start, doc_last)
            start = start + lengths[i]
        low = jnp.maximum(pos - (W - 1), doc_row) - (t0 - W)
        low2 = jnp.concatenate([low, low], axis=1)
        lane2 = jnp.concatenate([lane, lane], axis=1)

        def attend(count, packed):
            key_iota = lax.broadcasted_iota(jnp.int32, (TILE, 2 * TILE), 0)
            chunks = range(SPAN - count, SPAN)

            def scores_of(g):
                query = jnp.concatenate(
                    [
                        q_ref[:, 2 * g * HD : (2 * g + 1) * HD],
                        q_ref[:, (2 * g + 1) * HD : (2 * g + 2) * HD],
                    ],
                    axis=0,
                )
                scores = []
                for c in chunks:
                    key = kbuf[pl.ds(pl.multiple_of(off + c * TILE, TILE), TILE), g * HD : (g + 1) * HD]
                    s = lax.dot_general(
                        key, query, (((1,), (1,)), ((), ())), preferred_element_type=jnp.float32
                    )
                    if packed or c == 0:
                        s = jnp.where(key_iota >= low2 - c * TILE, s, MASKED)
                    if c == SPAN - 1:
                        s = jnp.where(key_iota <= lane2, s, MASKED)
                    scores.append(s)
                return scores

            def finish(g, scores):
                top = functools.reduce(
                    jnp.maximum, [jnp.max(s, axis=0, keepdims=True) for s in scores]
                )
                top2 = top * log2_scale
                total = jnp.zeros_like(top)
                mixed = jnp.zeros((HD, 2 * TILE), jnp.float32)
                for c, s in zip(chunks, scores):
                    p = jnp.exp2(s * log2_scale - top2)
                    total = total + jnp.sum(p, axis=0, keepdims=True)
                    value = vbuf[g * HD : (g + 1) * HD, pl.ds(pl.multiple_of(off + c * TILE, TILE), TILE)]
                    mixed = mixed + jnp.dot(
                        value, p.astype(jnp.bfloat16), preferred_element_type=jnp.float32
                    )
                mixed = mixed / total
                norm = top * score_scale + jnp.log(total)
                for half in range(2):
                    head = 2 * g + half
                    part = mixed[:, half * TILE : (half + 1) * TILE]
                    out_ref[:, head * HD : (head + 1) * HD] = part.T.astype(jnp.bfloat16)
                    norm_ref[head : head + 1, :] = norm[:, half * TILE : (half + 1) * TILE]

            every = [scores_of(g) for g in range(kv_heads)]
            for g in range(kv_heads):
                finish(g, every[g])

        skip = jnp.maximum(doc_first - (t0 - W), 0) // TILE
        plain = doc_last <= t0 - W + TILE

        @pl.when(plain)
        def _():
            attend(SPAN, False)

        few = skip >= SPAN - 3

        @pl.when(jnp.logical_not(plain) & few)
        def _():
            attend(3, True)

        @pl.when(jnp.logical_not(plain) & jnp.logical_not(few))
        def _():
            attend(SPAN, True)


def run_tiles(first, tiles, info, lengths, queries, keys, values, prefix_keys, prefix_values, carried):
    rows, query_width = queries.shape
    key_width = keys.shape[1]
    heads = query_width // HD
    per = BLK // TILE

    def moving(step, info, lengths):
        return (jnp.maximum(jnp.minimum(step + first, info[1] * per - 1), 0), 0)

    def out_map(step, info, lengths):
        return (step + first, 0)

    def norm_map(step, info, lengths):
        return (0, step + first)

    fixed = pl.BlockSpec((W, key_width), lambda step, info, lengths: (0, 0))
    in_specs = [
        pl.BlockSpec((TILE, query_width), moving),
        pl.BlockSpec((TILE, key_width), moving),
        pl.BlockSpec((TILE, key_width), moving),
        fixed,
        fixed,
    ]
    args = [queries, keys, values, prefix_keys, prefix_values]
    aliases = {}
    if carried:
        in_specs += [pl.BlockSpec(memory_space=pl.ANY)] * 2
        args += list(carried)
        aliases = {7: 0, 8: 1}
    length = W + tiles * TILE
    work = tiles * TILE * heads * (W + TILE)
    return pl.pallas_call(
        functools.partial(kernel, first, bool(carried)),
        out_shape=(
            jax.ShapeDtypeStruct((rows, query_width), jnp.bfloat16),
            jax.ShapeDtypeStruct((heads, rows), jnp.float32),
        ),
        grid_spec=pltpu.PrefetchScalarGridSpec(
            num_scalar_prefetch=2,
            grid=(tiles,),
            in_specs=in_specs,
            out_specs=[
                pl.BlockSpec((TILE, query_width), out_map),
                pl.BlockSpec((heads, TILE), norm_map),
            ],
            scratch_shapes=[
                pltpu.VMEM((length, key_width), jnp.bfloat16),
                pltpu.VMEM((key_width, length), jnp.bfloat16),
            ],
        ),
        input_output_aliases=aliases,
        compiler_params=pltpu.CompilerParams(
            dimension_semantics=("arbitrary",), vmem_limit_bytes=56 * 1024 * 1024
        ),
        cost_estimate=pl.CostEstimate(
            flops=4 * work * HD, transcendentals=work, bytes_accessed=4 * tiles * TILE * query_width
        ),
        name="window_attention",
    )(info, lengths, *args)


def local(queries, keys, values, doc_lengths, live_blocks):
    rows = queries.shape[0]
    shard = lax.axis_index("ctx")
    prev_keys, prev_values = from_behind((keys[rows - W :], values[rows - W :]), "ctx", 1)
    info = jnp.stack([shard * rows, live_blocks[shard]]).astype(jnp.int32)
    ahead = W // TILE
    carried = run_tiles(
        ahead, rows // TILE - ahead, info, doc_lengths, queries, keys, values, keys, values, None
    )
    return run_tiles(
        0, ahead, info, doc_lengths, queries, keys, values, prev_keys, prev_values, carried
    )


def solution(mesh):
    in_specs = (
        P(("groups", "ctx"), "head"),
        P(("groups", "ctx"), "head"),
        P(("groups", "ctx"), "head"),
        P("groups"),
        P("groups"),
    )
    out_specs = (P(("groups", "ctx"), "head"), P(("groups", "head"), "ctx"))
    return jax.shard_map(local, mesh=mesh, in_specs=in_specs, out_specs=out_specs, check_vma=False)
```

time: 277 us -> 95 us (0.34)
  matrix products: 86.6 us -> 0 us
  Pallas kernels: 0 us -> 78.7 us
  other arithmetic: 79.5 us -> 1.3 us
  local copies, waits for them, and re-layouts: 81.9 us -> 4.36 us
  loops' own time: 12.4 us -> 0 us
  waiting for transfers between devices: 5.61 us -> 0.01 us
    dot_general x32 -> x0, matrix products: 86.6 us -> none  [the longest x16 48.9 us: attend_block(): jnp.einsum('hgqk,khd->qhgd', weights, value_blk.reshape(span, kv_heads, H...]
    pallas_call x0 -> x2, Pallas kernels: none -> 78.7 us  [run_tiles(): pl.pallas_call(functools.partial(kernel, first, bool(carried)), out_shape...]
    reduce_sum x48 -> x0, other arithmetic: 46.6 us -> none  [the longest x16 43.7 us: attend_block(): total = jnp.sum(probs, axis=-1)]
    dynamic_slice x49 -> x1, local copies, waits for them, and re-layouts: 45.1 us -> 1.24 us  [local(): info = jnp.stack([shard * rows, live_blocks[shard]]).astype(jnp.int32)]
    and x16 -> x0, other arithmetic: 24.6 us -> none  [attend_block(): allowed & (key_pos[None, :] <= query_pos[:, None])]
    dynamic_update_slice x48 -> x0, local copies, waits for them, and re-layouts: 17 us -> none  [the longest x32 16.7 us: step_fn(): out_buf = lax.dynamic_update_slice(out_buf, attended, (index * BLK, 0))]
    unnamed x10 -> x4, local copies, waits for them, and re-layouts: 13.4 us -> 0.96 us
    another operation x1 -> x0, loops' own time: 12.4 us -> none  [run_blocks(): lax.fori_loop(jnp.int32(0), block_count, step_fn, (out_init, norm_init))]
  transfers between devices with their start and end apart: 2 -> 2, of which waited for: 1 -> 0; matrix products, arithmetic and copies ran while one was open for 5% -> 4% of each run, Pallas kernels for 0% -> 72%
where the time goes in v1:
time: 95 us; the launch traced here: 93.5 us
  Pallas kernels  78.7 us (83%)
  starting transfers between devices  8.47 us (9%)
  local copies, waits for them, and re-layouts  4.36 us (5%)
  other arithmetic  1.3 us (1%)
    pallas_call x2, Pallas kernels, run_tiles(): pl.pallas_call(functools.partial(kernel, first, bool(carried)), out_shape...  78.7 us
    ppermute x2, starting transfers between devices, from_behind(): return lax.ppermute(shard, axis, pairs)  8.47 us
  transfers between devices with their start and end apart: 2, of which 0 were waited for; matrix products, arithmetic and copies ran while one was open for 4% of the time, Pallas kernels for 72%

profile of v1, /device:TPU:0, one launch (start us, length us, event | category | flops | bytes accessed | tf_op | source)
XLA Modules:
  0.0 93.5 jit_solution(17681329115751283626)
XLA Ops:
  0.6 1.1 %slice.7 = bf16[1024,256]{1,0:T(8,128)(2,1)S(1)} slice(bf16[8192,256]{1,0:T(8,128)(2,1)} %v_ref.3), slice={[7168:8192], [0:256]} | slice | bytes 1048576 | tf_op jit(solution)/shard_map/slice | solution.py:201
  1.7 5.0 %collective-permute-start.1 = (bf16[1024,256]{1,0:T(8,128)(2,1)S(1)}, bf16[1024,256]{1,0:T(8,128)(2,1)S(1)}, u32[]{:S(2)}, u32[]{:S(2)}) collective-permute-start(bf16[1024,256]{1,0:T(8,128)(2,1)S(1)} %slice.7), channel_id=1, source_target_pairs={{0,4},{4,8},{8,12},{1,5},{5,9},{9,13},{2,6},{6,10},{10,14},{3,7},{... | collective-permute-start | bytes 1572872 | tf_op jit(solution)/shard_map/ppermute | solution.py:25
  6.7 1.1 %slice.6 = bf16[1024,256]{1,0:T(8,128)(2,1)S(1)} slice(bf16[8192,256]{1,0:T(8,128)(2,1)} %k_ref.3), slice={[7168:8192], [0:256]} | slice | bytes 1048576 | tf_op jit(solution)/shard_map/slice | solution.py:201
  7.8 3.5 %collective-permute-start = (bf16[1024,256]{1,0:T(8,128)(2,1)S(1)}, bf16[1024,256]{1,0:T(8,128)(2,1)S(1)}, u32[]{:S(2)}, u32[]{:S(2)}) collective-permute-start(bf16[1024,256]{1,0:T(8,128)(2,1)S(1)} %slice.6), channel_id=1, source_target_pairs={{0,4},{4,8},{8,12},{1,5},{5,9},{9,13},{2,6},{6,10},{10,14},{3,7},{... | collective-permute-start | bytes 1572872 | tf_op jit(solution)/shard_map/ppermute | solution.py:25
  11.3 1.2 %dynamic_slice.3 = s32[1]{0:T(128)} dynamic-slice(s32[4]{0:T(128)} %param.9, s32[]{:T(128)S(6)} %select_n.3), dynamic_slice_sizes={1} | dynamic-slice | bytes 12 | tf_op jit(solution)/shard_map/dynamic_slice | solution.py:202
  12.5 1.3 %pad_add_fusion.info = s32[2]{0:T(128)} fusion(s32[1]{0:T(128)} %dynamic_slice.3, s32[1]{0:T(128)} %bitcast), kind=kLoop, calls=%fused_computation | loop fusion | flops 2 | bytes 16 | tf_op jit(solution)/shard_map/stack | solution.py:202
  13.8 67.6 %window_attention.2 = (bf16[8192,512]{1,0:T(8,128)(2,1)}, f32[4,8192]{1,0:T(4,128)}) custom-call(s32[2]{0:T(128)} %pad_add_fusion.info, s32[16]{0:T(128)} %lengths.3, bf16[8192,512]{1,0:T(8,128)(2,1)} %q_ref.3, bf16[8192,256]{1,0:T(8,128)(2,1)} %k_ref.3, bf16[8192,256]{1,0:T(8,128)(2,1)} %v_ref.3, bf16[8192,256]{1,0:T(8,128)(2,1)} %k_ref.3, ...), custom_call_target="tpu_custom_call" | custom-call | flops 18790481920 | bytes 14680064 | tf_op jit(solution)/shard_map/window_attention/pallas_call | solution.py:168
  81.4 0.0 collective-permute-done.1.pv_ref
  81.4 0.0 copy-start
  81.4 0.0 collective-permute-done.pk_ref
  81.4 0.0 copy-start.1
  81.4 0.8 copy-done
  82.2 0.2 copy-done.1
  82.4 11.1 %window_attention.3 = (bf16[8192,512]{1,0:T(8,128)(2,1)}, f32[4,8192]{1,0:T(4,128)}) custom-call(s32[2]{0:T(128)} %pad_add_fusion.info, s32[16]{0:T(128)} %lengths.3, bf16[8192,512]{1,0:T(8,128)(2,1)} %q_ref.3, bf16[8192,256]{1,0:T(8,128)(2,1)} %k_ref.3, bf16[8192,256]{1,0:T(8,128)(2,1)} %v_ref.3, ...), custom_call_target="tpu_custom_call", output_to_operand_aliasing={{0}: (7, {}), {1}: (8, {})} | custom-call | flops 2684354560 | bytes 2097152 | tf_op jit(solution)/shard_map/window_attention/pallas_call | solution.py:168
Async XLA Ops:
  1.7 79.7 %collective-permute-start.1 = (bf16[1024,256]{1,0:T(8,128)(2,1)S(1)}, bf16[1024,256]{1,0:T(8,128)(2,1)S(1)}, u32[]{:S(2)}, u32[]{:S(2)}) collective-permute-start(bf16[1024,256]{1,0:T(8,128)(2,1)S(1)} %slice.7), channel_id=1, source_target_pairs={{0,4},{4,8},{8,12},{1,5},{5,9},{9,13},{2,6},{6,10},{10,14},{3,7},{... | collective-permute-start | bytes 1572872 | tf_op jit(solution)/shard_map/ppermute | solution.py:25
  7.8 73.6 %collective-permute-start = (bf16[1024,256]{1,0:T(8,128)(2,1)S(1)}, bf16[1024,256]{1,0:T(8,128)(2,1)S(1)}, u32[]{:S(2)}, u32[]{:S(2)}) collective-permute-start(bf16[1024,256]{1,0:T(8,128)(2,1)S(1)} %slice.6), channel_id=1, source_target_pairs={{0,4},{4,8},{8,12},{1,5},{5,9},{9,13},{2,6},{6,10},{10,14},{3,7},{... | collective-permute-start | bytes 1572872 | tf_op jit(solution)/shard_map/ppermute | solution.py:25
  81.4 0.8 copy-start
  81.4 1.0 %copy-start.1 = (bf16[1024,256]{1,0:T(8,128)(2,1)}, bf16[1024,256]{1,0:T(8,128)(2,1)S(1)}, u32[]{:S(2)}) copy-start(bf16[1024,256]{1,0:T(8,128)(2,1)S(1)} %collective-permute-done.pk_ref) | copy-start | bytes 1572868
